TPU v7x, 256 devices: a whole 4x4x8 slice. The times are simulated.
256 devices in a mesh: dp: 4 (over x), row: 8 (over z_lo, core), col: 8 (over z_hi, y).
Axes of the slice: x: 4, y: 4, z: 8 (z_hi: 2, z_lo: 4; z = z_hi * 4 + z_lo), core: 2. Of those that a mesh axis runs over, the one named last changes fastest.
Arguments:
- tokens: bfloat16 [4096, 8192], P(('dp', 'col'), 'row'), may hold values from -6 to 6
- gate_weight: bfloat16 [8192, 14336], P('row', ('dp', 'col')), may hold values from -0.0625 to 0.0625
- up_weight: bfloat16 [8192, 14336], P('row', ('dp', 'col')), may hold values from -0.0625 to 0.0625
- down_weight: bfloat16 [14336, 8192], P(('dp', 'col'), 'row'), may hold values from -0.046875 to 0.046875
Outputs:
- mixed: bfloat16 [4096, 8192], P(('dp', 'col'), 'row')
All inputs are finite; a program needn't handle non-finite values.
Results may differ from a plain program's by a relative error of at most 0.03.
Values may be sent and summed in bfloat16 or wider, within the bound.
A program may use at most 64 MiB of HBM per device.

v0:
```python
import jax
import jax.numpy as jnp
from jax import lax
from jax.sharding import PartitionSpec as P


def on_device(tokens, gate_weight, up_weight, down_weight):
    group_tokens = lax.all_gather(tokens, "col", axis=0, tiled=True)
    gate_cols, up_cols = (
        lax.all_gather(gate_weight, "dp", axis=1, tiled=True),
        lax.all_gather(up_weight, "dp", axis=1, tiled=True),
    )
    gate_term = jnp.dot(group_tokens, gate_cols, preferred_element_type=jnp.float32)
    up_term = jnp.dot(group_tokens, up_cols, preferred_element_type=jnp.float32)
    row_sums = lax.psum_scatter(
        jnp.concatenate((gate_term, up_term), axis=1).astype(jnp.bfloat16),
        "row",
        scatter_dimension=0,
        tiled=True,
    ).astype(jnp.float32)
    half_width = gate_cols.shape[1]
    gate_sum = row_sums[:, :half_width]
    up_sum = row_sums[:, half_width:]
    hidden = (jax.nn.silu(gate_sum) * up_sum).astype(jnp.bfloat16)
    hidden_all = lax.all_gather(hidden, "row", axis=0, tiled=True)
    down_term = jnp.dot(
        hidden_all,
        lax.all_gather(down_weight, "dp", axis=0, tiled=True),
        preferred_element_type=jnp.float32,
    )
    mixed = lax.psum_scatter(down_term.astype(jnp.bfloat16), "col", scatter_dimension=0, tiled=True)
    return mixed


def solution(mesh):
    return jax.shard_map(
        on_device,
        mesh=mesh,
        in_specs=(
            P(("dp", "col"), "row"),
            P("row", ("dp", "col")),
            P("row", ("dp", "col")),
            P(("dp", "col"), "row"),
        ),
        out_specs=P(("dp", "col"), "row"),
        check_vma=False,
    )
```

profile of v0, /device:TPU:2, one launch (start us, length us, event | category | flops | bytes accessed | tf_op | source)
XLA Modules:
  0.0 489.1 jit_solution(3508342044773073556)
XLA Ops:
  6.5 0.7 all-gather.6.cloned.1.call-update
  7.3 0.0 all-gather.8.cloned.1.call-start
  7.3 0.7 all-gather.8.cloned.1.call-update
  8.0 0.0 all-gather.10.cloned.1.call-start
  8.1 0.7 all-gather.10.cloned.1.call-update
  8.7 0.0 reduce-scatter.3.cloned.1.call-start
  8.8 80.1 %all-gather.6.cloned.1.call-done = bf16[1024,1024]{1,0:T(8,128)(2,1)} async-done(((bf16[128,1024]{1,0:T(8,128)(2,1)}), bf16[1024,1024]{1,0:T(8,128)(2,1)}) %all-gather.6.cloned.1.call-update) | async-done | bytes 2097168 | tf_op jit(solution)/shard_map/all_gather | solution.py:8
  88.9 43.2 %all-gather.8.cloned.1.call-done = bf16[1024,1792]{0,1:T(8,128)(2,1)} async-done(((bf16[1024,448]{0,1:T(8,128)(2,1)}), bf16[1024,1792]{0,1:T(8,128)(2,1)}) %all-gather.8.cloned.1.call-update) | async-done | bytes 3670032 | tf_op jit(solution)/shard_map/all_gather | solution.py:10
  132.1 8.5 %convolution_convert_fusion.1 = bf16[1024,1792]{1,0:T(8,128)(2,1)} fusion(bf16[1024,1024]{1,0:T(8,128)(2,1)} %all-gather.6.cloned.1.call-done, bf16[1024,1792]{0,1:T(8,128)(2,1)} %all-gather.8.cloned.1.call-done), kind=kOutput, calls=%fused_computation.2 | convolution fusion | flops 3759931392 | bytes 9437184 | tf_op jit(solution)/shard_map/dot_general | solution.py:13
  140.6 40.0 %all-gather.10.cloned.1.call-done = bf16[1024,1792]{0,1:T(8,128)(2,1)} async-done(((bf16[1024,448]{0,1:T(8,128)(2,1)}), bf16[1024,1792]{0,1:T(8,128)(2,1)}) %all-gather.10.cloned.1.call-update) | async-done | bytes 3670032 | tf_op jit(solution)/shard_map/all_gather | solution.py:11
  180.6 8.7 %convolution_convert_fusion = bf16[1024,1792]{1,0:T(8,128)(2,1)} fusion(bf16[1024,1024]{1,0:T(8,128)(2,1)} %all-gather.6.cloned.1.call-done, bf16[1024,1792]{0,1:T(8,128)(2,1)} %all-gather.10.cloned.1.call-done), kind=kOutput, calls=%fused_computation.1 | convolution fusion | flops 3759931392 | bytes 9437184 | tf_op jit(solution)/shard_map/dot_general | solution.py:14
  189.3 5.5 %pad_maximum_fusion = bf16[1024,3584]{1,0:T(8,128)(2,1)} fusion(bf16[1024,1792]{1,0:T(8,128)(2,1)} %convolution_convert_fusion, bf16[1024,1792]{1,0:T(8,128)(2,1)S(1)} %copy-done), kind=kLoop, calls=%fused_computation | loop fusion | flops 14680064 | bytes 14680064 | tf_op jit(solution)/shard_map/concatenate | solution.py:16
  194.8 0.0 reduce-scatter.3.cloned.1.call-update
  194.9 0.0 all-gather.14.cloned.1.call-start
  194.9 0.5 all-gather.14.cloned.1.call-update
  195.5 0.0 all-gather.12.cloned.1.call-start
  195.5 85.4 %reduce-scatter.3.cloned.1.call-done = bf16[128,3584]{1,0:T(8,128)(2,1)} async-done(((bf16[1024,3584]{1,0:T(8,128)(2,1)}), bf16[128,3584]{1,0:T(8,128)(2,1)}) %reduce-scatter.3.cloned.1.call-update) | async-done | bytes 917520 | tf_op jit(solution)/shard_map/reduce_scatter | solution.py:15
  280.9 1.4 convert_element_type.10
  282.3 1.0 fusion
  283.3 0.0 reduce-scatter.5.cloned.1.call-start
  283.4 43.5 %all-gather.14.cloned.1.call-done = bf16[1792,1024]{1,0:T(8,128)(2,1)} async-done(((bf16[448,1024]{1,0:T(8,128)(2,1)}), bf16[1792,1024]{1,0:T(8,128)(2,1)}) %all-gather.14.cloned.1.call-update) | async-done | bytes 3670032 | tf_op jit(solution)/shard_map/all_gather | solution.py:28
  326.9 52.3 %all-gather.12.cloned.1.call-done = bf16[1024,1792]{1,0:T(8,128)(2,1)} async-done(((bf16[128,1792]{1,0:T(8,128)(2,1)}), bf16[1024,1792]{1,0:T(8,128)(2,1)}) %all-gather.12.cloned.1.call-update) | async-done | bytes 3670032 | tf_op jit(solution)/shard_map/all_gather | solution.py:25
  379.2 8.4 %convolution_convert_fusion.2 = bf16[1024,1024]{1,0:T(8,128)(2,1)} fusion(bf16[1024,1792]{1,0:T(8,128)(2,1)} %all-gather.12.cloned.1.call-done, bf16[1792,1024]{1,0:T(8,128)(2,1)} %all-gather.14.cloned.1.call-done), kind=kOutput, calls=%fused_computation.3 | convolution fusion | flops 3759144960 | bytes 9437184 | tf_op jit(solution)/shard_map/dot_general | solution.py:26
  387.6 94.6 %reduce-scatter.5.cloned.1.call-done = bf16[128,1024]{1,0:T(8,128)(2,1)} async-done(((bf16[1024,1024]{1,0:T(8,128)(2,1)}), bf16[128,1024]{1,0:T(8,128)(2,1)}) %reduce-scatter.5.cloned.1.call-update) | async-done | bytes 262160 | tf_op jit(solution)/shard_map/reduce_scatter | solution.py:31
  (5 shorter events, 0.0 us)
Async XLA Ops:
  6.5 82.4 %all-gather.6.cloned.1.call-start = ((), (), s32[]{:S(2)}) async-start(), calls=%async_computation.2 | async-start | bytes 2359296 | tf_op jit(solution)/shard_map/all_gather | solution.py:8
  7.3 124.9 %all-gather.8.cloned.1.call-start = ((), (), s32[]{:S(2)}) async-start(), calls=%async_computation.3 | async-start | bytes 4587520 | tf_op jit(solution)/shard_map/all_gather | solution.py:10
  8.0 172.6 %all-gather.10.cloned.1.call-start = ((), (), s32[]{:S(2)}) async-start(), calls=%async_computation.4 | async-start | bytes 4587520 | tf_op jit(solution)/shard_map/all_gather | solution.py:11
  8.7 272.2 %reduce-scatter.3.cloned.1.call-start = ((), (), s32[]{:S(2)}) async-start(), calls=%async_computation.5 | async-start | bytes 8257536 | tf_op jit(solution)/shard_map/reduce_scatter | solution.py:15
  180.6 8.7 %copy-start = (bf16[1024,1792]{1,0:T(8,128)(2,1)S(1)}, bf16[1024,1792]{1,0:T(8,128)(2,1)}, u32[]{:S(2)}) copy-start(bf16[1024,1792]{1,0:T(8,128)(2,1)} %convolution_convert_fusion.1) | copy-start | bytes 11010052
  194.9 132.0 %all-gather.14.cloned.1.call-start = ((), (), s32[]{:S(2)}) async-start(), calls=%async_computation.7 | async-start | bytes 4587520 | tf_op jit(solution)/shard_map/all_gather | solution.py:28
  195.5 183.7 %all-gather.12.cloned.1.call-start = ((), (), s32[]{:S(2)}) async-start(), calls=%async_computation.6 | async-start | bytes 4128768 | tf_op jit(solution)/shard_map/all_gather | solution.py:25
  283.3 198.9 %reduce-scatter.5.cloned.1.call-start = ((), (), s32[]{:S(2)}) async-start(), calls=%async_computation.8 | async-start | bytes 2359296 | tf_op jit(solution)/shard_map/reduce_scatter | solution.py:31
Sparse Core Ops, SparseCore 0:
  10.0 78.8 all-gather.5
  90.7 41.3 all-gather.7
  133.9 46.6 all-gather.9
  195.0 85.8 reduce-scatter.2
  282.6 44.2 all-gather.13
  328.5 50.5 all-gather.11
  387.7 94.4 reduce-scatter.4
where the time goes:
time: 489 us
  waiting for transfers between devices  442 us (90%)
  matrix products  25.7 us (5%)
  between operations  13.5 us (3%)
  other arithmetic  7.89 us (2%)
    reduce_scatter x1, waiting for transfers between devices, on_device(): lax.psum_scatter(down_term.astype(jnp.bfloat16), 'col', scatter_dimension...  94.6 us
    reduce_scatter x1, waiting for transfers between devices, on_device(): lax.psum_scatter(jnp.concatenate((gate_term, up_term), axis=1).astype(jnp...  85.4 us
    all_gather x1, waiting for transfers between devices, on_device(): group_tokens = lax.all_gather(tokens, 'col', axis=0, tiled=True)  80.1 us
    all_gather x1, waiting for transfers between devices, on_device(): hidden_all = lax.all_gather(hidden, 'row', axis=0, tiled=True)  52.3 us
    all_gather x1, waiting for transfers between devices, on_device(): lax.all_gather(down_weight, 'dp', axis=0, tiled=True)  43.5 us
    all_gather x1, waiting for transfers between devices, on_device(): lax.all_gather(gate_weight, 'dp', axis=1, tiled=True)  43.2 us
    all_gather x1, waiting for transfers between devices, on_device(): lax.all_gather(up_weight, 'dp', axis=1, tiled=True)  40 us
  transfers between devices with their start and end apart: 7, of which 7 were waited for; matrix products, arithmetic and copies ran while one was open for 2% of the time, Pallas kernels for 0%

commit v1 on v0

v1 whole, which is shorter than its diff:
```python
import functools

import jax
import jax.numpy as jnp
from jax import lax
from jax.experimental import pallas as pl
from jax.experimental.pallas import tpu as pltpu
from jax.sharding import PartitionSpec as P

MESH = pl.DeviceIdType.MESH
F32 = jnp.float32
BF16 = jnp.bfloat16

CHUNKS = 2
BLOCK = 128
HALF = BLOCK // CHUNKS // 2
UNITS = 448
MAIN = 384
PACKED = 896
PADDED = 512
WIDTH = 1024
MESSAGES = 36


def kernel(tokens_ref, gate_ref, up_ref, down_ref, out_ref,
           tok, w, d, part, pair, chain_in, chain_out, hid, term,
           in_far, in_near, in_far2, in_near2, z_send, z_in,
           send_sem, recv_sem, local_sem):
    x = lax.axis_index("dp")
    row = lax.axis_index("row")
    col = lax.axis_index("col")
    z, core = row // 2, row % 2
    zh, y = col // 4, col % 4

    def shift(value, by):
        return lax.rem(value + (by + 4), 4)

    core_peer = {"row": row + 1 - 2 * core}
    zh_peer = {"col": (1 - zh) * 4 + y}
    x_peer = {1: {"dp": shift(x, 1)}, -1: {"dp": shift(x, -1)}}
    y_peer = {1: {"col": zh * 4 + shift(y, 1)}, -1: {"col": zh * 4 + shift(y, -1)}}

    barrier = pltpu.get_barrier_semaphore()
    for peer in (core_peer, zh_peer, x_peer[1], x_peer[-1], y_peer[1], y_peer[-1]):
        pl.semaphore_signal(barrier, inc=1, device_id=peer, device_id_type=MESH)

    @pl.when(z > 0)
    def _():
        pl.semaphore_signal(barrier, inc=1, device_id={"row": row - 2}, device_id_type=MESH)

    @pl.when(z < 3)
    def _():
        pl.semaphore_signal(barrier, inc=1, device_id={"row": row + 2}, device_id_type=MESH)

    at_end = jnp.logical_or(z == 0, z == 3)

    @pl.when(at_end)
    def _():
        pl.semaphore_wait(barrier, 7)

    @pl.when(jnp.logical_not(at_end))
    def _():
        pl.semaphore_wait(barrier, 8)

    sent = []

    def copy(src, dst, index, peer):
        return pltpu.make_async_remote_copy(
            src_ref=src, dst_ref=dst, send_sem=send_sem.at[index], recv_sem=recv_sem.at[index],
            device_id=peer, device_id_type=MESH)

    def send(src, dst, index, peer, guard=None):
        copy(src, dst, index, peer).start()
        sent.append((src, dst, index, peer, guard))

    def arrived(dst, index, peer):
        copy(dst, dst, index, peer).wait_recv()

    tasks = []

    def add(time, run, guard=None):
        tasks.append((time, len(tasks), run, guard))

    def one(c, o):
        base = (c * 2 + o) * MESSAGES
        first, second = (x, y) if o == 0 else (y, x)
        first_peer, second_peer = (x_peer, y_peer) if o == 0 else (y_peer, x_peer)
        lo = (c * 2 + o) * HALF
        mine = tokens_ref.at[pl.ds(lo, HALF)]
        here = tok.at[c, o]
        f = {k: shift(first, k) for k in (-1, 0, 1, 2)}
        s = {k: shift(second, k) for k in (-1, 0, 1, 2)}
        local = pltpu.make_async_copy(mine, here.at[s[0], f[0], zh], local_sem.at[c * 2 + o])
        t = lambda stage: TIMES[stage][c]

        def begin():
            send(mine, here.at[s[0], f[0], zh], base + 0, zh_peer)
            for i, way in enumerate((1, -1)):
                send(mine, here.at[s[0], f[0], zh], base + 1 + i, first_peer[way])
            local.start()

        def other_half():
            block = here.at[s[0], f[0], 1 - zh]
            arrived(block, base + 0, zh_peer)
            for i, way in enumerate((1, -1)):
                send(block, block, base + 3 + i, first_peer[way])

        def forward_own():
            block = here.at[s[0], f[-1], zh]
            arrived(block, base + 1, first_peer[-1])
            send(block, block, base + 5, first_peer[1])

        def forward_other():
            block = here.at[s[0], f[1], 1 - zh]
            arrived(block, base + 4, first_peer[1])
            send(block, block, base + 6, first_peer[-1])

        def second_axis():
            arrived(here.at[s[0], f[1], zh], base + 2, first_peer[1])
            arrived(here.at[s[0], f[-1], 1 - zh], base + 3, first_peer[-1])
            arrived(here.at[s[0], f[2], zh], base + 5, first_peer[-1])
            arrived(here.at[s[0], f[2], 1 - zh], base + 6, first_peer[1])
            local.wait()
            for i, way in enumerate((1, -1)):
                send(here.at[s[0]], here.at[s[0]], base + 7 + i, second_peer[way])

        def forward_second():
            arrived(here.at[s[-1]], base + 7, second_peer[-1])
            block = here.at[s[-1], 0:2]
            send(block, block, base + 9, second_peer[1])
            arrived(here.at[s[1]], base + 8, second_peer[1])
            block = here.at[s[1], 2:4]
            send(block, block, base + 10, second_peer[-1])

        add(t("begin"), begin)
        add(t("other_half"), other_half)
        add(t("forward_own"), forward_own)
        add(t("forward_other"), forward_other)
        add(t("second_axis"), second_axis)
        add(t("forward_second"), forward_second)

        p = z if o == 0 else 3 - z
        on = [p == position for position in range(4)]
        onward = {"row": row + 2} if o == 0 else {"row": row - 2}
        backward = {"row": row - 2} if o == 0 else {"row": row + 2}

        def tile(k):
            order = ORDER[c].index(k)
            key = k if k < 3 else -1
            rows = 4 * HALF
            own = part.at[c, o, k, :, core]
            away = part.at[c, o, k, :, 1 - core]
            pair_in = pair.at[c, o, k]
            incoming = chain_in.at[c, o, k]
            outgoing = chain_out.at[c, o, k]
            hidden = hid.at[c, o, k, core]
            hidden_away = hid.at[c, o, k, 1 - core]

            def gate_up():
                if k == 2:
                    arrived(here.at[s[2], 0:2], base + 9, second_peer[-1])
                    arrived(here.at[s[2], 2:4], base + 10, second_peer[1])
                a = here[s[key]].reshape(2 * rows, WIDTH)
                both = jnp.dot(a, w[...], preferred_element_type=F32).astype(BF16)
                part[c, o, k] = both.reshape(4, 2, HALF, PACKED)
                send(away, pair_in, base + 11 + k, core_peer)

            def total(with_chain):
                value = own[...].astype(F32).reshape(rows, PACKED) + pair_in[...].astype(F32).reshape(rows, PACKED)
                if with_chain:
                    value = value + incoming[...].astype(F32)
                return value

            def link(position):
                def run():
                    arrived(pair_in, base + 11 + k, core_peer)
                    if position:
                        arrived(incoming, base + 15 + k, backward)
                    value = total(position > 0)
                    if position < 3:
                        outgoing[...] = value.astype(BF16)
                        send(outgoing, incoming, base + 15 + k, onward, on[position])
                    else:
                        g, u = value[:, :MAIN], value[:, MAIN:2 * MAIN]
                        last = value[:, 2 * MAIN:]
                        turned = pltpu.roll(last, 64, 1)
                        lane = lax.broadcasted_iota(jnp.int32, last.shape, 1)
                        hidden[:, :MAIN] = (jax.nn.silu(g) * u).astype(BF16)
                        hidden[:, MAIN:] = jnp.where(lane < 64, jax.nn.silu(last) * turned, 0.0).astype(BF16)
                        send(hidden, hidden, base + 19 + k, backward, on[position])
                        send(hidden, hidden, base + 23 + k, core_peer, on[position])
                return run

            def spread(position):
                def run():
                    arrived(hidden, base + 19 + k, onward)
                    if position:
                        send(hidden, hidden, base + 19 + k, backward, on[position])
                    send(hidden, hidden, base + 23 + k, core_peer, on[position])
                return run

            def down():
                arrived(hidden_away, base + 23 + k, core_peer)
                a = hid[c, o, k].reshape(2 * rows, PADDED)
                term[c, o, k] = jnp.dot(a, d[...], preferred_element_type=F32).astype(BF16).reshape(2, 4, HALF, WIDTH)

            def out_far():
                for i, way in enumerate((1, -1)):
                    send(term.at[c, o, 2, i], in_far.at[c, o, i], base + 27 + i, second_peer[way])

            def out_near():
                i, way = (0, 1) if k == 1 else (1, -1)
                arrived(in_far.at[c, o, i], base + 27 + i, second_peer[-way])
                term[c, o, k, i] = (term[c, o, k, i].astype(F32) + in_far[c, o, i].astype(F32)).astype(BF16)
                send(term.at[c, o, k], in_near.at[c, o, i], base + 29 + i, second_peer[way])

            add(TIMES["gate_up"][c][order], gate_up)
            for position in range(4):
                add(TIMES["link"][c][order] + HOP * position, link(position), on[position])
            for position in (2, 1, 0):
                add(TIMES["link"][c][order] + HOP * 3 + SPREAD * (3 - position), spread(position), on[position])
            at = TIMES["down"][c][order]
            add(at, down)
            if k == 2:
                add(at + 0.1, out_far)
            elif k:
                add(max(at, TIMES["down"][c][ORDER[c].index(2)] + FAR) + 0.2, out_near)

        for k in ORDER[c]:
            tile(k)

        def out_second():
            for i, way in enumerate((1, -1)):
                arrived(in_near.at[c, o, i], base + 29 + i, second_peer[-way])
            value = term[c, o, 0].astype(F32) + in_near[c, o, 0].astype(F32) + in_near[c, o, 1].astype(F32)
            term[c, o, 0] = value.astype(BF16)
            for i, way in enumerate((1, -1)):
                send(term.at[c, o, 0, i, f[2]], in_far2.at[c, o, i], base + 31 + i, first_peer[way])

        def out_first():
            for i, way in enumerate((1, -1)):
                arrived(in_far2.at[c, o, i], base + 31 + i, first_peer[-way])
                block = term.at[c, o, 0, i, f[way]]
                block[...] = (block[...].astype(F32) + in_far2[c, o, i].astype(F32)).astype(BF16)
                send(term.at[c, o, 0, :, f[way]], in_near2.at[c, o, i], base + 33 + i, first_peer[way])

        def out_zh():
            for i, way in enumerate((1, -1)):
                arrived(in_near2.at[c, o, i], base + 33 + i, first_peer[-way])
            z_send[c, o] = (term[c, o, 0, :, f[0]].astype(F32) + in_near2[c, o, 0].astype(F32)
                            + in_near2[c, o, 1].astype(F32)).astype(BF16)
            send(z_send.at[c, o, 1 - zh], z_in.at[c, o], base + 35, zh_peer)

        def out_end():
            arrived(z_in.at[c, o], base + 35, zh_peer)
            out_ref[pl.ds(lo, HALF)] = (z_send[c, o, zh].astype(F32) + z_in[c, o].astype(F32)).astype(BF16)

        add(t("out_second"), out_second)
        add(t("out_first"), out_first)
        add(t("out_zh"), out_zh)
        add(t("out_end"), out_end)

    def pack():
        w[:, :MAIN] = gate_ref[:, :MAIN]
        w[:, MAIN:2 * MAIN] = up_ref[:, :MAIN]
        w[:, 2 * MAIN:] = jnp.concatenate((gate_ref[:, MAIN:], up_ref[:, MAIN:]), axis=1)
        d[:UNITS] = down_ref[...]
        d[UNITS:] = jnp.zeros((PADDED - UNITS, WIDTH), BF16)

    add(1.0, pack)
    for c in range(CHUNKS):
        for o in range(2):
            one(c, o)

    for _, _, run, guard in sorted(tasks, key=lambda task: task[:2]):
        if guard is None:
            run()
        else:
            pl.when(guard)(run)

    for src, dst, index, peer, guard in sent:
        def finish(item=(src, dst, index, peer)):
            copy(*item).wait_send()

        if guard is None:
            finish()
        else:
            pl.when(guard)(finish)


HOP = 7.0
SPREAD = 3.5
FAR = 8.0
ORDER = ((0, 1, 3, 2), (2, 1, 3, 0))
TIMES = {
    "begin": (0, 14),
    "other_half": (6, 20),
    "forward_own": (4, 18.5),
    "forward_other": (9, 22),
    "second_axis": (13, 27.5),
    "forward_second": (26, 46),
    "gate_up": ((14, 27, 28, 34), (53, 54, 55, 56)),
    "link": ((16, 28.5, 33, 38), (55, 58, 63, 68)),
    "down": ((49, 61, 66, 71), (89, 92, 97, 102)),
    "out_second": (92.5, 116),
    "out_first": (96, 120),
    "out_zh": (99, 124),
    "out_end": (105, 130),
}


def on_device(tokens, gate_weight, up_weight, down_weight):
    vmem = pl.BlockSpec(memory_space=pltpu.VMEM)
    c2 = (CHUNKS, 2)
    messages = CHUNKS * 2 * MESSAGES
    return pl.pallas_call(
        kernel,
        out_shape=jax.ShapeDtypeStruct(tokens.shape, BF16),
        in_specs=[vmem] * 4,
        out_specs=vmem,
        scratch_shapes=[
            pltpu.VMEM(c2 + (4, 4, 2, HALF, WIDTH), BF16),
            pltpu.VMEM((WIDTH, PACKED), BF16),
            pltpu.VMEM((PADDED, WIDTH), BF16),
            pltpu.VMEM(c2 + (4, 4, 2, HALF, PACKED), BF16),
            pltpu.VMEM(c2 + (4, 4, HALF, PACKED), BF16),
            pltpu.VMEM(c2 + (4, 4 * HALF, PACKED), BF16),
            pltpu.VMEM(c2 + (4, 4 * HALF, PACKED), BF16),
            pltpu.VMEM(c2 + (4, 2, 4 * HALF, PADDED), BF16),
            pltpu.VMEM(c2 + (4, 2, 4, HALF, WIDTH), BF16),
            pltpu.VMEM(c2 + (2, 4, HALF, WIDTH), BF16),
            pltpu.VMEM(c2 + (2, 2, 4, HALF, WIDTH), BF16),
            pltpu.VMEM(c2 + (2, HALF, WIDTH), BF16),
            pltpu.VMEM(c2 + (2, 2, HALF, WIDTH), BF16),
            pltpu.VMEM(c2 + (2, HALF, WIDTH), BF16),
            pltpu.VMEM(c2 + (HALF, WIDTH), BF16),
            pltpu.SemaphoreType.DMA((messages,)),
            pltpu.SemaphoreType.DMA((messages,)),
            pltpu.SemaphoreType.DMA((CHUNKS * 2,)),
        ],
        compiler_params=pltpu.CompilerParams(
            collective_id=0, has_side_effects=True, vmem_limit_bytes=63 * 1024 * 1024),
    )(tokens, gate_weight, up_weight, down_weight)


def solution(mesh):
    return jax.shard_map(
        on_device,
        mesh=mesh,
        in_specs=(
            P(("dp", "col"), "row"),
            P("row", ("dp", "col")),
            P("row", ("dp", "col")),
            P(("dp", "col"), "row"),
        ),
        out_specs=P(("dp", "col"), "row"),
        check_vma=False,
    )
```

time: 489 us -> 182 us (0.37)
  waiting for transfers between devices: 442 us -> 0 us
  Pallas kernels: 0 us -> 176 us
  matrix products: 25.7 us -> 0 us
  between operations: 13.5 us -> 0.01 us
  other arithmetic: 7.89 us -> 0 us
  local copies, waits for them, and re-layouts: 0.01 us -> 5.32 us
    all_gather x5 -> x0, waiting for transfers between devices: 259 us -> none  [the longest x1 80.1 us: on_device(): group_tokens = lax.all_gather(tokens, 'col', axis=0, tiled=True)]
    reduce_scatter x2 -> x0, waiting for transfers between devices: 180 us -> none  [the longest x1 94.6 us: on_device(): lax.psum_scatter(down_term.astype(jnp.bfloat16), 'col', scatter_dimension...]
    pallas_call x0 -> x1, Pallas kernels: none -> 176 us  [on_device(): pl.pallas_call(kernel, out_shape=jax.ShapeDtypeStruct(tokens.shape, BF16)...]
    dot_general x3 -> x0, matrix products: 25.7 us -> none  [the longest x1 8.71 us: on_device(): up_term = jnp.dot(group_tokens, up_cols, preferred_element_type=jnp.float32)]
    concatenate x1 -> x0, other arithmetic: 5.5 us -> none  [on_device(): jnp.concatenate((gate_term, up_term), axis=1).astype(jnp.bfloat16)]
    unnamed x2 -> x5, local copies, waits for them, and re-layouts: 0.01 us -> 5.32 us
  transfers between devices with their start and end apart: 7 -> 0, of which waited for: 7 -> 0; matrix products, arithmetic and copies ran while one was open for 2% -> 0% of each run, Pallas kernels for 0% -> 0%
where the time goes in v1:
time: 182 us
  Pallas kernels  176 us (97%)
  local copies, waits for them, and re-layouts  5.32 us (3%)
    pallas_call x1, Pallas kernels, on_device(): pl.pallas_call(kernel, out_shape=jax.ShapeDtypeStruct(tokens.shape, BF16)...  176 us
    unnamed x5, local copies, waits for them, and re-layouts  5.32 us

profile of v1, /device:TPU:2, one launch (start us, length us, event | category | flops | bytes accessed | tf_op | source)
XLA Modules:
  0.0 181.8 jit_solution(2819147080058547838)
XLA Ops:
  0.0 0.0 copy-start
  0.0 2.3 %copy.5.gate_ref = bf16[1024,448]{1,0:T(8,128)(2,1)} copy(bf16[1024,448]{0,1:T(8,128)(2,1)} %param.5) | data formatting | bytes 1835008 | tf_op args[1]
  2.3 0.0 copy-done
  2.3 1.3 copy.6.up_ref
  3.7 176.5 %shard_map.46 = bf16[128,1024]{1,0:T(8,128)(2,1)} custom-call(bf16[128,1024]{1,0:T(8,128)(2,1)} %tokens_ref.1, bf16[1024,448]{1,0:T(8,128)(2,1)} %copy.5.gate_ref, bf16[1024,448]{1,0:T(8,128)(2,1)} %copy.6.up_ref, bf16[448,1024]{1,0:T(8,128)(2,1)} %down_ref.1), custom_call_target="tpu_custom_call" | custom-call | tf_op jit(solution)/shard_map/pallas_call | solution.py:316
  180.1 1.7 copy.8
Async XLA Ops:
  0.0 2.3 %copy-start = (bf16[1024,448]{0,1:T(8,128)(2,1)S(1)}, bf16[1024,448]{0,1:T(8,128)(2,1)}, u32[]{:S(2)}) copy-start(bf16[1024,448]{0,1:T(8,128)(2,1)} %param.6) | copy-start | bytes 2752516

commit v2 on v1

v2 whole, which is shorter than its diff:
```python
import functools

import jax
import jax.numpy as jnp
from jax import lax
from jax.experimental import pallas as pl
from jax.experimental.pallas import tpu as pltpu
from jax.sharding import PartitionSpec as P

MESH = pl.DeviceIdType.MESH
F32 = jnp.float32
BF16 = jnp.bfloat16

CHUNKS = 4
BLOCK = 128
HALF = BLOCK // CHUNKS // 2
UNITS = 448
MAIN = 384
PACKED = 896
PADDED = 512
WIDTH = 1024
MESSAGES = 36


def kernel(tokens_ref, gate_ref, up_ref, down_ref, out_ref,
           tok, w, d, part, pair, chain_in, chain_out, hid, term,
           in_far, in_near, in_far2, in_near2, z_send, z_in,
           send_sem, recv_sem, local_sem):
    x = lax.axis_index("dp")
    row = lax.axis_index("row")
    col = lax.axis_index("col")
    z, core = row // 2, row % 2
    zh, y = col // 4, col % 4

    def shift(value, by):
        return lax.rem(value + (by + 4), 4)

    core_peer = {"row": row + 1 - 2 * core}
    zh_peer = {"col": (1 - zh) * 4 + y}
    def ring(by_x, by_y):
        return {"dp": lax.rem(x + (by_x + 4), 4), "col": zh * 4 + lax.rem(y + (by_y + 4), 4)}

    near = z // 2

    barrier = pltpu.get_barrier_semaphore()
    for peer in (core_peer, zh_peer, ring(1, 0), ring(-1, 0), ring(0, 1), ring(0, -1)):
        pl.semaphore_signal(barrier, inc=1, device_id=peer, device_id_type=MESH)

    @pl.when(z > 0)
    def _():
        pl.semaphore_signal(barrier, inc=1, device_id={"row": row - 2}, device_id_type=MESH)

    @pl.when(z < 3)
    def _():
        pl.semaphore_signal(barrier, inc=1, device_id={"row": row + 2}, device_id_type=MESH)

    at_end = jnp.logical_or(z == 0, z == 3)

    @pl.when(at_end)
    def _():
        pl.semaphore_wait(barrier, 7)

    @pl.when(jnp.logical_not(at_end))
    def _():
        pl.semaphore_wait(barrier, 8)

    sent = []

    def copy(src, dst, index, peer):
        place = index[0] + index[1]
        return pltpu.make_async_remote_copy(
            src_ref=src, dst_ref=dst, send_sem=send_sem.at[place], recv_sem=recv_sem.at[place],
            device_id=peer, device_id_type=MESH)

    def send(src, dst, index, peer, guard=None):
        copy(src, dst, index, peer).start()
        sent.append((src, dst, index, peer, guard))

    def arrived(dst, index, peer):
        copy(dst, dst, index, peer).wait_recv()

    tasks = []

    def add(run, guard=None):
        tasks.append((run, guard))

    def one(c, n):
        o = n + near - 2 * n * near
        swap = o
        base = (c * 2 + o) * MESSAGES
        first, second = x + swap * (y - x), y + swap * (x - y)
        first_peer = {way: ring((1 - swap) * way, swap * way) for way in (1, -1)}
        second_peer = {way: ring(swap * way, (1 - swap) * way) for way in (1, -1)}
        lo = pl.multiple_of((c * 2 + o) * HALF, HALF)
        mine = tokens_ref.at[pl.ds(lo, HALF)]
        here = tok.at[c, o]
        f = {k: shift(first, k) for k in (-1, 0, 1, 2)}
        s = {k: shift(second, k) for k in (-1, 0, 1, 2)}
        local = pltpu.make_async_copy(mine, here.at[s[0], f[0], zh], local_sem.at[c * 2 + o])

        def begin():
            send(mine, here.at[s[0], f[0], zh], (base, 0), zh_peer)
            for i, way in enumerate((1, -1)):
                send(mine, here.at[s[0], f[0], zh], (base, 1 + i), first_peer[way])
            local.start()

        def other_half():
            block = here.at[s[0], f[0], 1 - zh]
            arrived(block, (base, 0), zh_peer)
            for i, way in enumerate((1, -1)):
                send(block, block, (base, 3 + i), first_peer[way])

        def forward_own():
            block = here.at[s[0], f[-1], zh]
            arrived(block, (base, 1), first_peer[-1])
            send(block, block, (base, 5), first_peer[1])

        def forward_other():
            block = here.at[s[0], f[1], 1 - zh]
            arrived(block, (base, 4), first_peer[1])
            send(block, block, (base, 6), first_peer[-1])

        def second_axis():
            arrived(here.at[s[0], f[1], zh], (base, 2), first_peer[1])
            arrived(here.at[s[0], f[-1], 1 - zh], (base, 3), first_peer[-1])
            arrived(here.at[s[0], f[2], zh], (base, 5), first_peer[-1])
            arrived(here.at[s[0], f[2], 1 - zh], (base, 6), first_peer[1])
            local.wait()
            for i, way in enumerate((1, -1)):
                send(here.at[s[0]], here.at[s[0]], (base, 7 + i), second_peer[way])

        def forward_second(way):
            lower = 0 if way == 1 else 2

            def run():
                arrived(here.at[s[-way]], (base, (7 if way == 1 else 8)), second_peer[-way])
                block = here.at[s[-way], lower:lower + 2]
                send(block, block, (base, (9 if way == 1 else 10)), second_peer[way])

            return run

        add(begin)
        add(other_half)
        add(forward_own)
        add(forward_other)
        add(second_axis)
        add(forward_second(1))
        add(forward_second(-1))

        p = z + o * (3 - 2 * z)
        on = [p == position for position in range(4)]
        onward, backward = {"row": row + 2 - 4 * o}, {"row": row - 2 + 4 * o}

        def tile(k):
            key = k if k < 3 else -1
            rows = 4 * HALF
            own = part.at[c, o, k, :, core]
            away = part.at[c, o, k, :, 1 - core]
            pair_in = pair.at[c, o, k]
            incoming = chain_in.at[c, o, k]
            outgoing = chain_out.at[c, o, k]
            hidden = hid.at[c, o, k, core]
            hidden_away = hid.at[c, o, k, 1 - core]

            def gate_up():
                if k == 2:
                    arrived(here.at[s[2], 0:2], (base, 9), second_peer[-1])
                    arrived(here.at[s[2], 2:4], (base, 10), second_peer[1])
                a = here[s[key]].reshape(2 * rows, WIDTH)
                both = jnp.dot(a, w[...], preferred_element_type=F32).astype(BF16)
                part[c, o, k] = both.reshape(4, 2, HALF, PACKED)
                send(away, pair_in, (base, 11 + k), core_peer)

            def total(with_chain):
                value = own[...].astype(F32).reshape(rows, PACKED) + pair_in[...].astype(F32).reshape(rows, PACKED)
                if with_chain:
                    value = value + incoming[...].astype(F32)
                return value

            def link(position):
                def run():
                    arrived(pair_in, (base, 11 + k), core_peer)
                    if position:
                        arrived(incoming, (base, 15 + k), backward)
                    value = total(position > 0)
                    if position < 3:
                        outgoing[...] = value.astype(BF16)
                        send(outgoing, incoming, (base, 15 + k), onward, on[position])
                    else:
                        g, u = value[:, :MAIN], value[:, MAIN:2 * MAIN]
                        last = value[:, 2 * MAIN:]
                        turned = pltpu.roll(last, 64, 1)
                        lane = lax.broadcasted_iota(jnp.int32, last.shape, 1)
                        hidden[:, :MAIN] = (jax.nn.silu(g) * u).astype(BF16)
                        hidden[:, MAIN:] = jnp.where(lane < 64, jax.nn.silu(last) * turned, 0.0).astype(BF16)
                        send(hidden, hidden, (base, 19 + k), backward, on[position])
                        send(hidden, hidden, (base, 23 + k), core_peer, on[position])
                return run

            def spread(position):
                def run():
                    arrived(hidden, (base, 19 + k), onward)
                    if position:
                        send(hidden, hidden, (base, 19 + k), backward, on[position])
                    send(hidden, hidden, (base, 23 + k), core_peer, on[position])
                return run

            def down():
                arrived(hidden_away, (base, 23 + k), core_peer)
                a = hid[c, o, k].reshape(2 * rows, PADDED)
                term[c, o, k] = jnp.dot(a, d[...], preferred_element_type=F32).astype(BF16).reshape(2, 4, HALF, WIDTH)

            def out_far():
                for i, way in enumerate((1, -1)):
                    send(term.at[c, o, 2, i], in_far.at[c, o, i], (base, 27 + i), second_peer[way])

            def out_near():
                i, way = (0, 1) if k == 1 else (1, -1)
                arrived(in_far.at[c, o, i], (base, 27 + i), second_peer[-way])
                term[c, o, k, i] = (term[c, o, k, i].astype(F32) + in_far[c, o, i].astype(F32)).astype(BF16)
                send(term.at[c, o, k], in_near.at[c, o, i], (base, 29 + i), second_peer[way])

            add(gate_up)
            for position in range(2 - 2 * (1 - n), 4 - 2 * (1 - n)):
                add(link(position), on[position])
            for position in (2, 1, 0):
                if position // 2 == n:
                    add(spread(position), on[position])
            add(down)
            return out_far if k == 2 else out_near

        outs = [tile(k) for k in range(4)]
        for k in (2, 1, 3):
            add(outs[k])

        def out_second():
            for i, way in enumerate((1, -1)):
                arrived(in_near.at[c, o, i], (base, 29 + i), second_peer[-way])
            value = term[c, o, 0].astype(F32) + in_near[c, o, 0].astype(F32) + in_near[c, o, 1].astype(F32)
            term[c, o, 0] = value.astype(BF16)
            for i, way in enumerate((1, -1)):
                send(term.at[c, o, 0, i, f[2]], in_far2.at[c, o, i], (base, 31 + i), first_peer[way])

        def out_first():
            for i, way in enumerate((1, -1)):
                arrived(in_far2.at[c, o, i], (base, 31 + i), first_peer[-way])
                block = term.at[c, o, 0, i, f[way]]
                block[...] = (block[...].astype(F32) + in_far2[c, o, i].astype(F32)).astype(BF16)
                send(term.at[c, o, 0, :, f[way]], in_near2.at[c, o, i], (base, 33 + i), first_peer[way])

        def out_zh():
            for i, way in enumerate((1, -1)):
                arrived(in_near2.at[c, o, i], (base, 33 + i), first_peer[-way])
            z_send[c, o] = (term[c, o, 0, :, f[0]].astype(F32) + in_near2[c, o, 0].astype(F32)
                            + in_near2[c, o, 1].astype(F32)).astype(BF16)
            send(z_send.at[c, o, 1 - zh], z_in.at[c, o], (base, 35), zh_peer)

        def out_end():
            arrived(z_in.at[c, o], (base, 35), zh_peer)
            out_ref[pl.ds(lo, HALF)] = (z_send[c, o, zh].astype(F32) + z_in[c, o].astype(F32)).astype(BF16)

        add(out_second)
        add(out_first)
        add(out_zh)
        add(out_end)

    def pack():
        w[:, :MAIN] = gate_ref[:, :MAIN]
        w[:, MAIN:2 * MAIN] = up_ref[:, :MAIN]
        w[:, 2 * MAIN:] = jnp.concatenate((gate_ref[:, MAIN:], up_ref[:, MAIN:]), axis=1)
        d[:UNITS] = down_ref[...]
        d[UNITS:] = jnp.zeros((PADDED - UNITS, WIDTH), BF16)

    for c in range(CHUNKS):
        for n in range(2):
            one(c, n)
    for place, number in enumerate(ORDER):
        if place == PACK:
            pack()
        run, guard = tasks[number]
        if guard is None:
            run()
        else:
            pl.when(guard)(run)

    for src, dst, index, peer, guard in sent:
        def finish(item=(src, dst, index, peer)):
            copy(*item).wait_send()

        if guard is None:
            finish()
        else:
            pl.when(guard)(finish)


PACK = 4
ORDER = (
    0, 38, 182, 110, 72, 216, 144, 2, 74, 112, 254, 256, 40, 1, 39, 3, 218, 146, 183, 41,
    111, 73, 4, 7, 8, 75, 184, 145, 217, 113, 255, 185, 76, 79, 80, 147, 42, 45, 9, 46,
    5, 81, 6, 13, 14, 15, 148, 151, 152, 186, 189, 219, 25, 26, 47, 114, 117, 44, 50, 51,
    118, 27, 153, 77, 97, 98, 19, 20, 257, 78, 85, 86, 99, 43, 60, 48, 49, 61, 149, 169,
    170, 52, 91, 92, 21, 150, 157, 158, 220, 223, 224, 116, 122, 115, 132, 62, 171, 55, 56, 57,
    163, 164, 258, 261, 133, 134, 93, 87, 187, 204, 205, 127, 188, 194, 119, 159, 128, 129, 206, 221,
    241, 242, 222, 229, 260, 266, 123, 124, 58, 59, 65, 63, 64, 22, 165, 199, 259, 195, 196, 135,
    235, 236, 120, 23, 24, 31, 28, 29, 53, 54, 66, 200, 201, 207, 208, 190, 191, 243, 67, 121,
    100, 130, 131, 137, 16, 17, 276, 230, 172, 125, 30, 33, 271, 18, 32, 225, 101, 102, 277, 278,
    94, 95, 96, 103, 202, 203, 209, 237, 262, 173, 174, 166, 167, 136, 139, 231, 126, 138, 88, 89,
    168, 175, 263, 105, 211, 272, 273, 90, 104, 197, 198, 210, 267, 268, 177, 68, 82, 83, 192, 193,
    160, 140, 161, 162, 176, 10, 11, 274, 275, 281, 84, 106, 12, 34, 238, 239, 240, 247, 154, 269,
    212, 279, 280, 283, 270, 282, 232, 155, 156, 178, 69, 141, 233, 234, 248, 244, 245, 246, 249, 35,
    264, 265, 284, 226, 107, 108, 213, 179, 142, 70, 227, 228, 250, 36, 214, 285, 251, 180, 286, 252,
    215, 109, 181, 143, 71, 287, 253, 37,
)


def on_device(tokens, gate_weight, up_weight, down_weight):
    vmem = pl.BlockSpec(memory_space=pltpu.VMEM)
    c2 = (CHUNKS, 2)
    messages = CHUNKS * 2 * MESSAGES
    return pl.pallas_call(
        kernel,
        out_shape=jax.ShapeDtypeStruct(tokens.shape, BF16),
        in_specs=[vmem] * 4,
        out_specs=vmem,
        scratch_shapes=[
            pltpu.VMEM(c2 + (4, 4, 2, HALF, WIDTH), BF16),
            pltpu.VMEM((WIDTH, PACKED), BF16),
            pltpu.VMEM((PADDED, WIDTH), BF16),
            pltpu.VMEM(c2 + (4, 4, 2, HALF, PACKED), BF16),
            pltpu.VMEM(c2 + (4, 4, HALF, PACKED), BF16),
            pltpu.VMEM(c2 + (4, 4 * HALF, PACKED), BF16),
            pltpu.VMEM(c2 + (4, 4 * HALF, PACKED), BF16),
            pltpu.VMEM(c2 + (4, 2, 4 * HALF, PADDED), BF16),
            pltpu.VMEM(c2 + (4, 2, 4, HALF, WIDTH), BF16),
            pltpu.VMEM(c2 + (2, 4, HALF, WIDTH), BF16),
            pltpu.VMEM(c2 + (2, 2, 4, HALF, WIDTH), BF16),
            pltpu.VMEM(c2 + (2, HALF, WIDTH), BF16),
            pltpu.VMEM(c2 + (2, 2, HALF, WIDTH), BF16),
            pltpu.VMEM(c2 + (2, HALF, WIDTH), BF16),
            pltpu.VMEM(c2 + (HALF, WIDTH), BF16),
            pltpu.SemaphoreType.DMA((messages,)),
            pltpu.SemaphoreType.DMA((messages,)),
            pltpu.SemaphoreType.DMA((CHUNKS * 2,)),
        ],
        compiler_params=pltpu.CompilerParams(
            collective_id=0, has_side_effects=True, vmem_limit_bytes=63 * 1024 * 1024),
    )(tokens, gate_weight, up_weight, down_weight)


def solution(mesh):
    return jax.shard_map(
        on_device,
        mesh=mesh,
        in_specs=(
            P(("dp", "col"), "row"),
            P("row", ("dp", "col")),
            P("row", ("dp", "col")),
            P(("dp", "col"), "row"),
        ),
        out_specs=P(("dp", "col"), "row"),
        check_vma=False,
    )
```

time: 182 us -> 149 us (0.82)
  Pallas kernels: 176 us -> 143 us
    pallas_call x1, Pallas kernels: 176 us -> 143 us  [on_device(): pl.pallas_call(kernel, out_shape=jax.ShapeDtypeStruct(tokens.shape, BF16)...]
where the time goes in v2:
time: 149 us
  Pallas kernels  143 us (96%)
  local copies, waits for them, and re-layouts  5.32 us (4%)
    pallas_call x1, Pallas kernels, on_device(): pl.pallas_call(kernel, out_shape=jax.ShapeDtypeStruct(tokens.shape, BF16)...  143 us
    unnamed x5, local copies, waits for them, and re-layouts  5.32 us

profile of v2, /device:TPU:2, one launch (start us, length us, event | category | flops | bytes accessed | tf_op | source)
XLA Modules:
  0.0 148.7 jit_solution(9735880550424358011)
XLA Ops:
  0.0 0.0 copy-start
  0.0 2.3 %copy.5.gate_ref = bf16[1024,448]{1,0:T(8,128)(2,1)} copy(bf16[1024,448]{0,1:T(8,128)(2,1)} %param.5) | data formatting | bytes 1835008 | tf_op args[1]
  2.3 0.0 copy-done
  2.3 1.3 copy.6.up_ref
  3.7 143.3 %shard_map.46 = bf16[128,1024]{1,0:T(8,128)(2,1)} custom-call(bf16[128,1024]{1,0:T(8,128)(2,1)} %tokens_ref.1, bf16[1024,448]{1,0:T(8,128)(2,1)} %copy.5.gate_ref, bf16[1024,448]{1,0:T(8,128)(2,1)} %copy.6.up_ref, bf16[448,1024]{1,0:T(8,128)(2,1)} %down_ref.1), custom_call_target="tpu_custom_call" | custom-call | tf_op jit(solution)/shard_map/pallas_call | solution.py:320
  147.0 1.7 %copy.8 = bf16[128,1024]{1,0:T(8,128)(2,1)} copy(bf16[128,1024]{1,0:T(8,128)(2,1)} %shard_map.46) | data formatting | bytes 524288
Async XLA Ops:
  0.0 2.3 %copy-start = (bf16[1024,448]{0,1:T(8,128)(2,1)S(1)}, bf16[1024,448]{0,1:T(8,128)(2,1)}, u32[]{:S(2)}) copy-start(bf16[1024,448]{0,1:T(8,128)(2,1)} %param.6) | copy-start | bytes 2752516

commit v3 on v2

--- a/solution.py
+++ b/solution.py
@@ -15,6 +15,7 @@
 BLOCK = 128
 HALF = BLOCK // CHUNKS // 2
 UNITS = 448
+TAIL = 64
 MAIN = 384
 PACKED = 896
 PADDED = 512
@@ -22,10 +23,12 @@
 MESSAGES = 36
 
 
-def kernel(tokens_ref, gate_ref, up_ref, down_ref, out_ref,
-           tok, w, d, part, pair, chain_in, chain_out, hid, term,
+def kernel(tokens_hbm, gate_hbm, up_hbm, down_hbm, out_hbm,
+           tokens_ref, out_ref, weights, tok, w, d, part, pair, chain_in, chain_out, hid, term,
            in_far, in_near, in_far2, in_near2, z_send, z_in,
-           send_sem, recv_sem, local_sem):
+           send_sem, recv_sem, local_sem, load_sem, store_sem):
+    load_tokens = pltpu.make_async_copy(tokens_hbm, tokens_ref, load_sem.at[0])
+    load_tokens.start()
     x = lax.axis_index("dp")
     row = lax.axis_index("row")
     col = lax.axis_index("col")
@@ -54,6 +57,20 @@
     def _():
         pl.semaphore_signal(barrier, inc=1, device_id={"row": row + 2}, device_id_type=MESH)
 
+    loads = [
+        pltpu.make_async_copy(src, dst, load_sem.at[1 + i])
+        for i, (src, dst) in enumerate((
+            (gate_hbm.at[:MAIN], weights.at[:MAIN]),
+            (up_hbm.at[:MAIN], weights.at[MAIN:2 * MAIN]),
+            (gate_hbm.at[MAIN:], weights.at[2 * MAIN:2 * MAIN + TAIL]),
+            (up_hbm.at[MAIN:], weights.at[2 * MAIN + TAIL:]),
+            (down_hbm, d.at[:UNITS]),
+        ))
+    ]
+    for load in loads:
+        load.start()
+    d[UNITS:] = jnp.zeros((PADDED - UNITS, WIDTH), BF16)
+
     at_end = jnp.logical_or(z == 0, z == 3)
 
     @pl.when(at_end)
@@ -64,7 +81,9 @@
     def _():
         pl.semaphore_wait(barrier, 8)
 
+    load_tokens.wait()
     sent = []
+    stores = []
 
     def copy(src, dst, index, peer):
         place = index[0] + index[1]
@@ -190,9 +209,13 @@
                         g, u = value[:, :MAIN], value[:, MAIN:2 * MAIN]
                         last = value[:, 2 * MAIN:]
                         turned = pltpu.roll(last, 64, 1)
-                        lane = lax.broadcasted_iota(jnp.int32, last.shape, 1)
-                        hidden[:, :MAIN] = (jax.nn.silu(g) * u).astype(BF16)
-                        hidden[:, MAIN:] = jnp.where(lane < 64, jax.nn.silu(last) * turned, 0.0).astype(BF16)
+                        lane = lax.broadcasted_iota(jnp.int32, (rows // 2, 128), 1)
+                        main = (jax.nn.silu(g) * u).astype(BF16)
+                        for j in range(3):
+                            hidden[2 * j:2 * j + 2] = main[:, j * 128:(j + 1) * 128].reshape(2, rows // 2, 128)
+                        tail = jax.nn.silu(last) * turned
+                        other = pltpu.roll(tail[rows // 2:], 64, 1)
+                        hidden[6] = jnp.where(lane < TAIL, tail[:rows // 2], other).astype(BF16)
                         send(hidden, hidden, (base, 19 + k), backward, on[position])
                         send(hidden, hidden, (base, 23 + k), core_peer, on[position])
                 return run
@@ -207,7 +230,14 @@
 
             def down():
                 arrived(hidden_away, (base, 23 + k), core_peer)
-                a = hid[c, o, k].reshape(2 * rows, PADDED)
+                halves = []
+                for h in range(2):
+                    tail = hid[c, o, k, h, 6]
+                    other = pltpu.roll(tail.astype(F32), 64, 1).astype(BF16)
+                    tiles = [hid[c, o, k, h, 2 * j:2 * j + 2].reshape(rows, 128) for j in range(3)]
+                    tiles.append(jnp.concatenate((tail, other), axis=0))
+                    halves.append(jnp.concatenate(tiles, axis=1))
+                a = jnp.concatenate(halves, axis=0)
                 term[c, o, k] = jnp.dot(a, d[...], preferred_element_type=F32).astype(BF16).reshape(2, 4, HALF, WIDTH)
 
             def out_far():
@@ -257,7 +287,11 @@
 
         def out_end():
             arrived(z_in.at[c, o], (base, 35), zh_peer)
-            out_ref[pl.ds(lo, HALF)] = (z_send[c, o, zh].astype(F32) + z_in[c, o].astype(F32)).astype(BF16)
+            rows = pl.ds(lo, HALF)
+            out_ref[rows] = (z_send[c, o, zh].astype(F32) + z_in[c, o].astype(F32)).astype(BF16)
+            store = (out_ref.at[rows], out_hbm.at[rows], store_sem.at[c * 2 + o])
+            pltpu.make_async_copy(*store).start()
+            stores.append(store)
 
         add(out_second)
         add(out_first)
@@ -265,11 +299,15 @@
         add(out_end)
 
     def pack():
-        w[:, :MAIN] = gate_ref[:, :MAIN]
-        w[:, MAIN:2 * MAIN] = up_ref[:, :MAIN]
-        w[:, 2 * MAIN:] = jnp.concatenate((gate_ref[:, MAIN:], up_ref[:, MAIN:]), axis=1)
-        d[:UNITS] = down_ref[...]
-        d[UNITS:] = jnp.zeros((PADDED - UNITS, WIDTH), BF16)
+        for load in loads:
+            load.wait()
+
+        def turn(i, carry):
+            start = pl.multiple_of(i * 128, 128)
+            w[:, pl.ds(start, 128)] = weights[pl.ds(start, 128), :].T
+            return carry
+
+        lax.fori_loop(0, PACKED // 128, turn, 0)
 
     for c in range(CHUNKS):
         for n in range(2):
@@ -283,6 +321,8 @@
         else:
             pl.when(guard)(run)
 
+    for store in stores:
+        pltpu.make_async_copy(*store).wait()
     for src, dst, index, peer, guard in sent:
         def finish(item=(src, dst, index, peer)):
             copy(*item).wait_send()
@@ -295,34 +335,37 @@
 
 PACK = 4
 ORDER = (
-    0, 38, 182, 110, 72, 216, 144, 2, 74, 112, 254, 256, 40, 1, 39, 3, 218, 146, 183, 41,
-    111, 73, 4, 7, 8, 75, 184, 145, 217, 113, 255, 185, 76, 79, 80, 147, 42, 45, 9, 46,
-    5, 81, 6, 13, 14, 15, 148, 151, 152, 186, 189, 219, 25, 26, 47, 114, 117, 44, 50, 51,
-    118, 27, 153, 77, 97, 98, 19, 20, 257, 78, 85, 86, 99, 43, 60, 48, 49, 61, 149, 169,
-    170, 52, 91, 92, 21, 150, 157, 158, 220, 223, 224, 116, 122, 115, 132, 62, 171, 55, 56, 57,
-    163, 164, 258, 261, 133, 134, 93, 87, 187, 204, 205, 127, 188, 194, 119, 159, 128, 129, 206, 221,
-    241, 242, 222, 229, 260, 266, 123, 124, 58, 59, 65, 63, 64, 22, 165, 199, 259, 195, 196, 135,
-    235, 236, 120, 23, 24, 31, 28, 29, 53, 54, 66, 200, 201, 207, 208, 190, 191, 243, 67, 121,
-    100, 130, 131, 137, 16, 17, 276, 230, 172, 125, 30, 33, 271, 18, 32, 225, 101, 102, 277, 278,
-    94, 95, 96, 103, 202, 203, 209, 237, 262, 173, 174, 166, 167, 136, 139, 231, 126, 138, 88, 89,
-    168, 175, 263, 105, 211, 272, 273, 90, 104, 197, 198, 210, 267, 268, 177, 68, 82, 83, 192, 193,
-    160, 140, 161, 162, 176, 10, 11, 274, 275, 281, 84, 106, 12, 34, 238, 239, 240, 247, 154, 269,
-    212, 279, 280, 283, 270, 282, 232, 155, 156, 178, 69, 141, 233, 234, 248, 244, 245, 246, 249, 35,
-    264, 265, 284, 226, 107, 108, 213, 179, 142, 70, 227, 228, 250, 36, 214, 285, 251, 180, 286, 252,
-    215, 109, 181, 143, 71, 287, 253, 37,
+    0, 72, 38, 110, 182, 144, 146, 216, 112, 184, 254, 1, 2, 218, 40, 74, 256, 3, 73, 39,
+    41, 111, 75, 4, 7, 8, 183, 145, 147, 9, 113, 217, 76, 79, 80, 42, 45, 46, 5, 25,
+    26, 185, 6, 13, 14, 81, 148, 255, 27, 151, 152, 114, 117, 47, 15, 77, 43, 97, 98, 60,
+    19, 20, 78, 85, 86, 48, 44, 50, 49, 51, 149, 169, 170, 186, 99, 116, 150, 157, 158, 219,
+    21, 61, 118, 257, 87, 115, 91, 92, 52, 122, 153, 132, 133, 62, 55, 163, 258, 171, 188, 56,
+    164, 57, 220, 223, 224, 194, 123, 124, 93, 187, 204, 127, 205, 206, 63, 64, 28, 29, 259, 134,
+    58, 165, 128, 129, 222, 229, 221, 241, 242, 53, 10, 189, 22, 159, 23, 199, 24, 31, 200, 59,
+    201, 65, 125, 235, 261, 207, 260, 266, 236, 16, 190, 17, 191, 130, 225, 131, 137, 30, 33, 135,
+    18, 32, 54, 172, 230, 88, 66, 89, 195, 196, 202, 203, 209, 67, 94, 95, 243, 126, 138, 136,
+    139, 271, 166, 237, 167, 119, 96, 276, 103, 100, 277, 101, 278, 208, 211, 168, 231, 175, 90, 104,
+    192, 102, 105, 272, 273, 197, 198, 210, 160, 161, 173, 174, 177, 162, 176, 120, 267, 268, 193, 121,
+    140, 82, 83, 274, 68, 275, 281, 238, 11, 12, 34, 262, 239, 240, 247, 212, 279, 280, 283, 269,
+    270, 282, 141, 263, 244, 245, 69, 84, 106, 232, 233, 213, 246, 249, 234, 248, 154, 155, 156, 178,
+    35, 264, 265, 284, 226, 214, 70, 142, 179, 227, 107, 36, 228, 250, 180, 285, 251, 108, 286, 252,
+    143, 215, 181, 109, 71, 287, 37, 253,
 )
 
 
 def on_device(tokens, gate_weight, up_weight, down_weight):
-    vmem = pl.BlockSpec(memory_space=pltpu.VMEM)
+    hbm = pl.BlockSpec(memory_space=pl.ANY)
     c2 = (CHUNKS, 2)
     messages = CHUNKS * 2 * MESSAGES
     return pl.pallas_call(
         kernel,
         out_shape=jax.ShapeDtypeStruct(tokens.shape, BF16),
-        in_specs=[vmem] * 4,
-        out_specs=vmem,
+        in_specs=[hbm] * 4,
+        out_specs=hbm,
         scratch_shapes=[
+            pltpu.VMEM((BLOCK, WIDTH), BF16),
+            pltpu.VMEM((BLOCK, WIDTH), BF16),
+            pltpu.VMEM((PACKED, WIDTH), BF16),
             pltpu.VMEM(c2 + (4, 4, 2, HALF, WIDTH), BF16),
             pltpu.VMEM((WIDTH, PACKED), BF16),
             pltpu.VMEM((PADDED, WIDTH), BF16),
@@ -330,7 +373,7 @@
             pltpu.VMEM(c2 + (4, 4, HALF, PACKED), BF16),
             pltpu.VMEM(c2 + (4, 4 * HALF, PACKED), BF16),
             pltpu.VMEM(c2 + (4, 4 * HALF, PACKED), BF16),
-            pltpu.VMEM(c2 + (4, 2, 4 * HALF, PADDED), BF16),
+            pltpu.VMEM(c2 + (4, 2, 7, 2 * HALF, 128), BF16),
             pltpu.VMEM(c2 + (4, 2, 4, HALF, WIDTH), BF16),
             pltpu.VMEM(c2 + (2, 4, HALF, WIDTH), BF16),
             pltpu.VMEM(c2 + (2, 2, 4, HALF, WIDTH), BF16),
@@ -341,10 +384,12 @@
             pltpu.SemaphoreType.DMA((messages,)),
             pltpu.SemaphoreType.DMA((messages,)),
             pltpu.SemaphoreType.DMA((CHUNKS * 2,)),
+            pltpu.SemaphoreType.DMA((6,)),
+            pltpu.SemaphoreType.DMA((CHUNKS * 2,)),
         ],
         compiler_params=pltpu.CompilerParams(
             collective_id=0, has_side_effects=True, vmem_limit_bytes=63 * 1024 * 1024),
-    )(tokens, gate_weight, up_weight, down_weight)
+    )(tokens, gate_weight.T, up_weight.T, down_weight)
 
 
 def solution(mesh):

time: 149 us -> 140 us (0.940)
  Pallas kernels: 143 us -> 138 us
  local copies, waits for them, and re-layouts: 5.32 us -> 1.67 us
    pallas_call x1, Pallas kernels: 143 us -> 138 us  [on_device(): pl.pallas_call(kernel, out_shape=jax.ShapeDtypeStruct(tokens.shape, BF16)...]
    unnamed x5 -> x1, local copies, waits for them, and re-layouts: 5.32 us -> 1.67 us
where the time goes in v3:
time: 140 us
  Pallas kernels  138 us (99%)
  local copies, waits for them, and re-layouts  1.67 us (1%)
    pallas_call x1, Pallas kernels, on_device(): pl.pallas_call(kernel, out_shape=jax.ShapeDtypeStruct(tokens.shape, BF16)...  138 us

profile of v3, /device:TPU:2, one launch (start us, length us, event | category | flops | bytes accessed | tf_op | source)
XLA Modules:
  0.0 139.5 jit_solution(1090608044589941567)
XLA Ops:
  0.0 137.8 %shard_map.46 = bf16[128,1024]{1,0:T(8,128)(2,1)} custom-call(bf16[128,1024]{1,0:T(8,128)(2,1)} %tokens_hbm.1, bf16[448,1024]{1,0:T(8,128)(2,1)} %bitcast.2, bf16[448,1024]{1,0:T(8,128)(2,1)} %bitcast.3, bf16[448,1024]{1,0:T(8,128)(2,1)} %down_hbm.1), custom_call_target="tpu_custom_call" | custom-call | tf_op jit(solution)/shard_map/pallas_call | solution.py:360
  137.9 1.7 %copy.6 = bf16[128,1024]{1,0:T(8,128)(2,1)} copy(bf16[128,1024]{1,0:T(8,128)(2,1)} %shard_map.46) | data formatting | bytes 524288
